TPU v7x, 512 devices: a whole 4x8x8 slice. The times are simulated.
512 devices in a mesh: rep: 32 (over x, y), tp: 16 (over z, core).
Axes of the slice: x: 4, y: 8, z: 8, core: 2. Of those that a mesh axis runs over, the one named last changes fastest.
Arguments:
- queries: bfloat16 [416, 48, 4096], P('rep', None, 'tp'), may hold values from -33 to 33
- tree_cache: bfloat16 [416, 2, 48, 4096], P('rep', None, None, 'tp'), may hold values from -11 to 11
- tree_mask: int32 [416, 48, 48], P('rep'), may hold values from 0 to 1, as said below
- dest_group: int32 [416, 1], P('rep'), may hold values from 0 to 31; in each aligned block of 13 rows (0 to 12, 13 to 25, ...) at most 2 rows name the same one
- accepted_path: int32 [416, 8], P('rep'), may hold values from 0 to 47
- prompt_cache: bfloat16 [32, 2, 152, 4096], P('rep', None, None, 'tp'), may hold values from -11 to 11
- first_len: int32 [32], P('rep'), may hold values from 2 to 152
- spill_cache: bfloat16 [32, 2, 152, 4096], P('rep', None, None, 'tp'), may hold values from -6 to 6
- spill_len: int32 [32], P('rep'), may hold values from 76 to 152
- out_weight: bfloat16 [4096, 4096], P(None, 'tp'), may hold values from -0.09375 to 0.09375
Outputs:
- projected: bfloat16 [416, 48, 4096], P('rep', None, 'tp')
- accepted_cache: bfloat16 [416, 2, 8, 4096], P('rep', None, None, 'tp')
Inputs may be any that keep to these rules, and one draw needn't show every extreme that they name: `dest_group`: in each aligned block of 13 requests (those of one index of rep) no group is named more than 2 times. Row t of tree_mask[r] marks token t and its ancestors in a tree whose parents come before their children.
All inputs are finite; a program needn't handle non-finite values.
Results may differ from a plain program's by a relative error of at most 0.014.
Values may be sent and summed in bfloat16 or wider, within the bound.
A program may use at most 64 MiB of HBM per device.

v0:
```python
import math
import jax
import jax.numpy as jnp
from jax import lax
from jax.sharding import PartitionSpec as P

HD = 128
TREE = 48
PCAP = 152
NEG_FILL = -1e30


def swapped(value, axis, apart):
    mask = 2**apart
    pairs = [(source, source ^ mask) for source in range(lax.axis_size(axis))]
    return lax.ppermute(value, axis, pairs)


def attend_part(query_rows, key_rows, value_rows, visible, head_size):
    heads_here = query_rows.shape[2] // head_size
    maxima = []
    totals = []
    partial_sums = []
    for head_index in range(heads_here):
        lower = head_index * head_size
        upper = lower + head_size
        scores = lax.dot_general(
            query_rows[:, :, lower:upper],
            key_rows[:, :, lower:upper],
            (((2,), (2,)), ((0,), (0,))),
            preferred_element_type=jnp.float32,
        ) * (1.0 / math.sqrt(head_size))
        scores = jnp.where(visible, scores, NEG_FILL)
        peaks = jnp.max(scores, axis=2)
        raw_weights = jnp.where(visible, jnp.exp(scores - peaks[:, :, None]), 0.0)
        maxima.append(peaks)
        totals.append(jnp.sum(raw_weights, axis=2))
        partial_sums.append(
            lax.dot_general(
                raw_weights.astype(jnp.bfloat16),
                value_rows[:, :, lower:upper],
                (((2,), (1,)), ((0,), (0,))),
                preferred_element_type=jnp.float32,
            )
        )
    return (
        jnp.stack(maxima, axis=-1),
        jnp.stack(totals, axis=-1),
        jnp.concatenate(partial_sums, axis=-1),
    )


def combine_parts(first_part, second_part, head_size):
    max_first, total_first, accum_first = first_part
    max_second, total_second, accum_second = second_part
    peaks = jnp.maximum(max_first, max_second)
    factor_first = jnp.exp(max_first - peaks)
    factor_second = jnp.exp(max_second - peaks)
    totals = total_first * factor_first + total_second * factor_second
    full_shape = accum_first.shape
    split_shape = full_shape[:-1] + (full_shape[-1] // head_size, head_size)
    accum = (
        accum_first.reshape(split_shape) * factor_first[..., None]
        + accum_second.reshape(split_shape) * factor_second[..., None]
    )
    return (peaks, totals, accum.reshape(full_shape))


def local(
    queries,
    tree_cache,
    tree_mask,
    dest_group,
    accepted_path,
    prompt_cache,
    first_len,
    spill_cache,
    spill_len,
    out_weight,
):
    req_here = queries.shape[0]
    local_cols = queries.shape[2]
    heads_here = local_cols // HD
    groups = lax.axis_size("rep")
    per_group = max(2, (req_here + groups - 1) // groups)
    n_slots = groups * per_group
    target = dest_group[:, 0]
    same_target = target[:, None] == target[None, :]
    earlier = jnp.arange(req_here)[None, :] < jnp.arange(req_here)[:, None]
    rank_index = jnp.sum(jnp.logical_and(same_target, earlier), axis=1)
    slot_index = target * per_group + rank_index
    selector = (jnp.arange(n_slots, dtype=jnp.int32)[:, None] == slot_index[None, :]).astype(
        jnp.bfloat16
    )
    outbound = jnp.einsum(
        "sr,rtc->stc", selector, queries, preferred_element_type=jnp.float32
    ).astype(jnp.bfloat16)
    outbound = outbound.reshape(groups, per_group, TREE, local_cols)
    inbound = lax.all_to_all(outbound, "rep", split_axis=0, concat_axis=0, tiled=True)
    routed_rows = inbound.reshape(1, n_slots * TREE, local_cols)
    positions = jnp.arange(PCAP, dtype=jnp.int32)
    prompt_seen = (positions < first_len[0])[None, None, :]
    prompt_part = attend_part(routed_rows, prompt_cache[:, 0], prompt_cache[:, 1], prompt_seen, HD)
    live_flag = (positions < spill_len[0]).astype(jnp.bfloat16)
    partner_cache, partner_flag = swapped((spill_cache, live_flag), "rep", 0)
    spill_seen = (partner_flag > 0.5)[None, None, :]
    spill_part = attend_part(routed_rows, partner_cache[:, 0], partner_cache[:, 1], spill_seen, HD)
    merged_max, merged_total, merged_accum = combine_parts(prompt_part, spill_part, HD)
    back_max, back_total, back_accum = (
        lax.all_to_all(
            merged_max.reshape(groups, per_group, TREE, heads_here),
            "rep",
            split_axis=0,
            concat_axis=0,
            tiled=True,
        ),
        lax.all_to_all(
            merged_total.reshape(groups, per_group, TREE, heads_here),
            "rep",
            split_axis=0,
            concat_axis=0,
            tiled=True,
        ),
        lax.all_to_all(
            merged_accum.reshape(groups, per_group, TREE, local_cols),
            "rep",
            split_axis=0,
            concat_axis=0,
            tiled=True,
        ),
    )
    remote_part = (
        jnp.take(back_max.reshape(n_slots, TREE, heads_here), slot_index, axis=0),
        jnp.take(back_total.reshape(n_slots, TREE, heads_here), slot_index, axis=0),
        jnp.take(back_accum.reshape(n_slots, TREE, local_cols), slot_index, axis=0),
    )
    tree_seen = tree_mask == 1
    tree_part = attend_part(queries, tree_cache[:, 0], tree_cache[:, 1], tree_seen, HD)
    final_max, final_total, final_accum = combine_parts(remote_part, tree_part, HD)
    attn = final_accum.reshape(req_here, TREE, heads_here, HD) / final_total[..., None]
    attn = attn.reshape(req_here * TREE, local_cols).astype(jnp.bfloat16)
    summed = jnp.dot(
        lax.all_gather(attn, "tp", axis=1, tiled=True),
        out_weight,
        preferred_element_type=jnp.float32,
    )
    projected = summed.astype(jnp.bfloat16).reshape(req_here, TREE, out_weight.shape[1])
    accepted_cache = jnp.take_along_axis(tree_cache, accepted_path[:, None, :, None], axis=2)
    return (projected, accepted_cache)


def solution(mesh):
    return jax.shard_map(
        local,
        mesh=mesh,
        in_specs=(
            P("rep", None, "tp"),
            P("rep", None, None, "tp"),
            P("rep", None, None),
            P("rep", None),
            P("rep", None),
            P("rep", None, None, "tp"),
            P("rep"),
            P("rep", None, None, "tp"),
            P("rep"),
            P(None, "tp"),
        ),
        out_specs=(P("rep", None, "tp"), P("rep", None, None, "tp")),
        check_vma=False,
    )
```

profile of v0, /device:TPU:1, one launch (start us, length us, event | category | flops | bytes accessed | tf_op | source)
XLA Modules:
  0.0 319.3 jit_solution(14354112950949048452)
XLA Ops:
  7.2 1.0 convert_reduce_fusion
  8.2 1.1 compare_and_fusion.1
  9.3 1.7 convolution_convert_fusion
  11.0 2.0 copy.131
  13.0 10.7 %all-to-all-start = ((bf16[32,2,48,256]{3,2,1,0:T(8,128)(2,1)}), bf16[32,2,48,256]{3,2,1,0:T(8,128)(2,1)}, u32[]{:S(2)}, u32[]{:S(2)}) async-start(bf16[32,2,48,256]{3,2,1,0:T(8,128)(2,1)} %bitcast.162), calls=%async_computation | async-start | bytes 3145728 | tf_op jit(solution)/shard_map/all_to_all | solution.py:99
  23.8 3.1 collective-permute-start.1
  27.5 2.2 collective-permute-start
  30.5 31.8 %collective-permute-done = bf16[152]{0:T(256)(128)(2,1)S(1)} collective-permute-done((bf16[152]{0:T(256)(128)(2,1)S(1)}, bf16[152]{0:T(256)(128)(2,1)S(1)}, u32[]{:S(2)}, u32[]{:S(2)}) %collective-permute-start) | collective-permute-done | bytes 336 | tf_op jit(solution)/shard_map/ppermute | solution.py:16
  62.3 3.1 fusion.59
  65.3 3.1 fusion.60
  68.4 3.1 fusion.57
  71.5 3.0 fusion.58
  74.8 3.8 %fusion.9 = (f32[3072]{0:T(1024)S(1)}, f32[3072]{0:T(1024)S(1)}, bf16[3072,152]{0,1:T(8,128)(2,1)S(1)}, bf16[3072,152]{0,1:T(8,128)(2,1)}) fusion(f32[3072,152]{0,1:T(8,128)} %get-tuple-element.47, f32[3072]{0:T(1024)S(1)} %get-tuple-element.46, pred[152]{0:T(512)(128)(4,1)S(1)} %broadcast_compare_fusion.1, f32[3072,152]{0,1:T(8,128)} %get-tuple-element.49, ...), kind=kLoop, calls=%fused_computation.24 | loop fusion | flops 3729408 | bytes 5652632 | tf_op jit(solution)/shard_map/reduce_sum | solution.py:37
  78.5 2.5 copy.100
  81.0 1.6 copy.99
  82.5 3.3 %fusion.38 = f32[32,2,48,128]{3,2,1,0:T(8,128)} fusion(bf16[32,2,48,152]{3,2,1,0:T(8,128)(2,1)} %bitcast.166, bf16[1,152,256]{2,1,0:T(8,128)(2,1)S(1)} %get-tuple-element.32), kind=kOutput, calls=%fused_computation.74 | convolution fusion | flops 119537664 | bytes 2545664 | tf_op jit(solution)/shard_map/dot_general | solution.py:39
  85.8 1.7 fusion.39
  87.7 3.7 %fusion.5 = (f32[3072]{0:T(1024)S(1)}, f32[3072]{0:T(1024)S(1)}, bf16[3072,152]{0,1:T(8,128)(2,1)S(1)}, bf16[3072,152]{0,1:T(8,128)(2,1)}) fusion(f32[3072,152]{0,1:T(8,128)} %get-tuple-element.43, f32[3072]{0:T(1024)S(1)} %get-tuple-element.42, pred[152]{0:T(512)(128)(4,1)S(1)} %iota_compare_fusion.2, f32[3072,152]{0,1:T(8,128)} %get-tuple-element.45, ...), kind=kLoop, calls=%fused_computation.20 | loop fusion | flops 3729408 | bytes 5652632 | tf_op jit(solution)/shard_map/reduce_sum | solution.py:37
  91.4 2.5 copy.97
  93.9 1.5 copy.96
  96.8 9.2 %all-to-all-start.2 = ((f32[32,1,192]{2,1,0:T(1,128)}), f32[32,1,192]{2,1,0:T(1,128)S(1)}, u32[]{:S(2)}, u32[]{:S(2)}) async-start(f32[32,1,192]{2,1,0:T(1,128)} %reshape.496), calls=%async_computation.2 | async-start | bytes 65536 | tf_op jit(solution)/shard_map/all_to_all | solution.py:110
  106.1 3.3 %fusion.40 = f32[32,2,48,128]{3,2,1,0:T(8,128)} fusion(bf16[32,2,48,152]{3,2,1,0:T(8,128)(2,1)} %bitcast.164, bf16[1,152,256]{2,1,0:T(8,128)(2,1)S(1)} %get-tuple-element.34), kind=kOutput, calls=%fused_computation.80 | convolution fusion | flops 119537664 | bytes 2545664 | tf_op jit(solution)/shard_map/dot_general | solution.py:39
  109.4 1.7 fusion.41
  111.1 1.7 copy.98
  112.8 8.1 %mul.105 = f32[3072,2,128]{2,1,0:T(2,128)} broadcast(f32[3072,2]{1,0:T(8,128)} %copy.98), dimensions={0,1} | broadcast | bytes 3170304 | tf_op jit(solution)/shard_map/mul | solution.py:63
  120.9 5.5 %mul.106 = f32[32,2,48,256]{3,2,1,0:T(8,128)} reshape(f32[3072,2,128]{2,1,0:T(2,128)} %mul.105) | data formatting | bytes 6291456 | tf_op jit(solution)/shard_map/mul | solution.py:63
  126.4 1.7 copy.101
  128.1 8.1 %mul.108 = f32[3072,2,128]{2,1,0:T(2,128)} broadcast(f32[3072,2]{1,0:T(8,128)} %copy.101), dimensions={0,1} | broadcast | bytes 3170304 | tf_op jit(solution)/shard_map/mul | solution.py:64
  136.2 5.5 %mul.109 = f32[32,2,48,256]{3,2,1,0:T(8,128)} reshape(f32[3072,2,128]{2,1,0:T(2,128)} %mul.108) | data formatting | bytes 6291456 | tf_op jit(solution)/shard_map/mul | solution.py:64
  142.6 9.1 %all-to-all-start.3 = ((f32[32,1,192]{2,1,0:T(1,128)}), f32[32,1,192]{2,1,0:T(1,128)S(1)}, u32[]{:S(2)}, u32[]{:S(2)}) async-start(f32[32,1,192]{2,1,0:T(1,128)} %reshape.498), calls=%async_computation.3 | async-start | bytes 65536 | tf_op jit(solution)/shard_map/all_to_all | solution.py:117
  151.6 7.4 %fusion.4 = f32[32,2,48,256]{3,2,1,0:T(8,128)} fusion(f32[32,2,48,256]{3,2,1,0:T(8,128)} %mul.106, f32[32,2,48,128]{3,2,1,0:T(8,128)} %fusion.40, f32[32,2,48,128]{3,2,1,0:T(8,128)} %fusion.41, f32[32,2,48,256]{3,2,1,0:T(8,128)} %mul.109, f32[32,2,48,128]{3,2,1,0:T(8,128)} %fusion.38, f32[32,2,48,128]{3,2,1,0:T(8,128)} %fusion.39), kind=kLoop, calls=%fused_computation.13 | loop fusion | flops 3932160 | bytes 15728640 | tf_op jit(solution)/shard_map/add | solution.py:63
  159.0 1.4 all-to-all-done.3
  161.0 8.0 %all-to-all-start.1 = ((f32[32,2,48,256]{3,2,1,0:T(8,128)}), f32[32,2,48,256]{3,2,1,0:T(8,128)}, u32[]{:S(2)}, u32[]{:S(2)}) async-start(f32[32,2,48,256]{3,2,1,0:T(8,128)} %fusion.4), calls=%async_computation.1 | async-start | bytes 6291456 | tf_op jit(solution)/shard_map/all_to_all | solution.py:124
  169.6 1.2 fusion.55
  170.7 1.3 fusion.56
  175.9 1.2 fusion.22
  177.1 1.2 fusion.24
  179.8 1.5 reduce.16
  185.2 0.9 copy.110
  186.1 0.9 copy.114
  187.9 51.7 %all-to-all-done.1 = f32[32,2,48,256]{3,2,1,0:T(8,128)} async-done(((f32[32,2,48,256]{3,2,1,0:T(8,128)}), f32[32,2,48,256]{3,2,1,0:T(8,128)}, u32[]{:S(2)}, u32[]{:S(2)}) %all-to-all-start.1) | async-done | bytes 3145760 | tf_op jit(solution)/shard_map/all_to_all | solution.py:124
  239.6 3.4 %gather_fusion = f32[13,48,256]{2,1,0:T(8,128)} fusion(f32[64,48,256]{2,1,0:T(8,128)} %bitcast.38, s32[1024]{0:T(1024)} %pad_clamp_fusion.1), kind=kCustom, calls=%fused_computation.2 | custom fusion | bytes 1278004 | tf_op jit(solution)/shard_map/jit(_take)/gather | solution.py:135
  243.0 1.8 mul.113
  244.9 1.7 mul.116
  247.5 1.0 fusion.15
  248.7 1.6 gather_fusion.1
  251.2 56.6 %all-gather.2.cloned.1.call-done = bf16[624,4096]{1,0:T(8,128)(2,1)} async-done(((bf16[624,256]{1,0:T(8,128)(2,1)}), bf16[624,4096]{1,0:T(8,128)(2,1)}) %all-gather.2.cloned.1.call-update) | async-done | bytes 5111824 | tf_op jit(solution)/shard_map/all_gather | solution.py:143
  307.8 4.7 %convolution_convert_fusion.1 = bf16[624,256]{1,0:T(8,128)(2,1)} fusion(bf16[624,4096]{1,0:T(8,128)(2,1)} %all-gather.2.cloned.1.call-done, bf16[4096,256]{1,0:T(8,128)(2,1)S(1)} %copy-done), kind=kOutput, calls=%fused_computation.28 | convolution fusion | flops 1308782592 | bytes 7528448 | tf_op jit(solution)/shard_map/dot_general | solution.py:142
  (94 shorter events, 15.7 us)
Async XLA Ops:
  7.2 300.6 %copy-start = (bf16[4096,256]{1,0:T(8,128)(2,1)S(1)}, bf16[4096,256]{1,0:T(8,128)(2,1)}, u32[]{:S(2)}) copy-start(bf16[4096,256]{1,0:T(8,128)(2,1)} %param.21) | copy-start | bytes 6291460
  13.0 10.8 %copy-start.14 = (bf16[1,2,152,256]{3,2,1,0:T(8,128)(2,1)S(1)}, bf16[1,2,152,256]{3,2,1,0:T(8,128)(2,1)}, u32[]{:S(2)}) copy-start(bf16[1,2,152,256]{3,2,1,0:T(8,128)(2,1)} %param.19) | copy-start | bytes 466948
  13.0 17.4 %copy-start.9 = (bf16[1,2,152,256]{3,2,1,0:T(8,128)(2,1)S(1)}, bf16[1,2,152,256]{3,2,1,0:T(8,128)(2,1)}, u32[]{:S(2)}) copy-start(bf16[1,2,152,256]{3,2,1,0:T(8,128)(2,1)} %param.17) | copy-start | bytes 466948
  13.0 49.2 %all-to-all-start = ((bf16[32,2,48,256]{3,2,1,0:T(8,128)(2,1)}), bf16[32,2,48,256]{3,2,1,0:T(8,128)(2,1)}, u32[]{:S(2)}, u32[]{:S(2)}) async-start(bf16[32,2,48,256]{3,2,1,0:T(8,128)(2,1)} %bitcast.162), calls=%async_computation | async-start | bytes 3145728 | tf_op jit(solution)/shard_map/all_to_all | solution.py:99
  23.8 38.4 %collective-permute-start.1 = (bf16[1,2,152,256]{3,2,1,0:T(8,128)(2,1)S(1)}, bf16[1,2,152,256]{3,2,1,0:T(8,128)(2,1)S(1)}, u32[]{:S(2)}, u32[]{:S(2)}) collective-permute-start(bf16[1,2,152,256]{3,2,1,0:T(8,128)(2,1)S(1)} %copy-done.14), channel_id=1, source_target_pairs={{0,16},{16,0},{32,48},{48,32},{64,80},{80,64},{96,112},{112,96},{1... | collective-permute-start | bytes 466952 | tf_op jit(solution)/shard_map/ppermute | solution.py:16
  27.5 34.7 %collective-permute-start = (bf16[152]{0:T(256)(128)(2,1)S(1)}, bf16[152]{0:T(256)(128)(2,1)S(1)}, u32[]{:S(2)}, u32[]{:S(2)}) collective-permute-start(bf16[152]{0:T(256)(128)(2,1)S(1)} %compare_convert_fusion), channel_id=1, source_target_pairs={{0,16},{16,0},{32,48},{48,32},{64,80},{80,64},{96,112},{112,96},{1... | collective-permute-start | bytes 920 | tf_op jit(solution)/shard_map/ppermute | solution.py:16
  82.5 3.3 %copy-start.2 = (bf16[3072,152]{1,0:T(8,128)(2,1)S(1)}, bf16[3072,152]{1,0:T(8,128)(2,1)}, u32[]{:S(2)}) copy-start(bf16[3072,152]{1,0:T(8,128)(2,1)} %copy.99) | copy-start | bytes 2801668
  96.8 45.7 %all-to-all-start.2 = ((f32[32,1,192]{2,1,0:T(1,128)}), f32[32,1,192]{2,1,0:T(1,128)S(1)}, u32[]{:S(2)}, u32[]{:S(2)}) async-start(f32[32,1,192]{2,1,0:T(1,128)} %reshape.496), calls=%async_computation.2 | async-start | bytes 65536 | tf_op jit(solution)/shard_map/all_to_all | solution.py:110
  106.1 3.4 %copy-start.1 = (bf16[3072,152]{1,0:T(8,128)(2,1)S(1)}, bf16[3072,152]{1,0:T(8,128)(2,1)}, u32[]{:S(2)}) copy-start(bf16[3072,152]{1,0:T(8,128)(2,1)} %copy.96) | copy-start | bytes 2801668
  142.6 17.8 %all-to-all-start.3 = ((f32[32,1,192]{2,1,0:T(1,128)}), f32[32,1,192]{2,1,0:T(1,128)S(1)}, u32[]{:S(2)}, u32[]{:S(2)}) async-start(f32[32,1,192]{2,1,0:T(1,128)} %reshape.498), calls=%async_computation.3 | async-start | bytes 65536 | tf_op jit(solution)/shard_map/all_to_all | solution.py:117
  159.0 10.2 %copy-start.8 = (s32[13,48,48]{2,1,0:T(8,128)S(1)}, s32[13,48,48]{2,1,0:T(8,128)}, u32[]{:S(2)}) copy-start(s32[13,48,48]{2,1,0:T(8,128)} %param.14) | copy-start | bytes 359428
  159.0 10.5 %copy-start.3 = (bf16[13,2,48,256]{3,2,1,0:T(8,128)(2,1)S(1)}, bf16[13,2,48,256]{3,2,1,0:T(8,128)(2,1)}, u32[]{:S(2)}) copy-start(bf16[13,2,48,256]{3,2,1,0:T(8,128)(2,1)} %param.13) | copy-start | bytes 1916932
  160.4 0.6 copy-start.10
  161.0 78.6 %all-to-all-start.1 = ((f32[32,2,48,256]{3,2,1,0:T(8,128)}), f32[32,2,48,256]{3,2,1,0:T(8,128)}, u32[]{:S(2)}, u32[]{:S(2)}) async-start(f32[32,2,48,256]{3,2,1,0:T(8,128)} %fusion.4), calls=%async_computation.1 | async-start | bytes 6291456 | tf_op jit(solution)/shard_map/all_to_all | solution.py:124
  169.0 138.8 %all-gather.2.cloned.1.call-start = ((), (), s32[]{:S(2)}) async-start(), calls=%async_computation.4 | async-start | bytes 5431296 | tf_op jit(solution)/shard_map/all_gather | solution.py:143
  169.5 4.4 %copy-start.13 = (s32[13,1]{0,1:T(1,128)S(1)}, s32[13,1]{0,1:T(1,128)}, u32[]{:S(2)}) copy-start(s32[13,1]{0,1:T(1,128)} %param.15) | copy-start | bytes 160
  170.7 1.5 copy-start.5
  172.0 0.7 copy-start.6
  239.6 7.9 %copy-start.12 = (pred[624]{0:T(1024)(128)(4,1)S(1)}, pred[624]{0:T(1024)(128)(4,1)}, u32[]{:S(2)}) copy-start(pred[624]{0:T(1024)(128)(4,1)} %broadcast_in_dim.103) | copy-start | bytes 1876
  243.0 3.6 %copy-start.7 = (f32[13,48,2]{2,1,0:T(8,128)S(1)}, f32[13,48,2]{2,1,0:T(8,128)}, u32[]{:S(2)}) copy-start(f32[13,48,2]{2,1,0:T(8,128)} %copy.121) | copy-start | bytes 14980
  243.0 4.4 %copy-start.4 = (f32[13,48,256]{2,1,0:T(8,128)S(1)}, f32[13,48,256]{2,1,0:T(8,128)}, u32[]{:S(2)}) copy-start(f32[13,48,256]{2,1,0:T(8,128)} %gather_fusion) | copy-start | bytes 1916932
  247.5 1.0 copy-start.11
Sparse Core Ops, SparseCore 0:
  248.6 59.1 all-gather.1
where the time goes:
time: 321 us; the launch traced here: 319 us
  waiting for transfers between devices  141 us (44%)
  local copies, waits for them, and re-layouts  63.3 us (20%)
  starting transfers between devices  42.5 us (13%)
  matrix products  33.4 us (10%)
  other arithmetic  22.8 us (7%)
  between operations  15.8 us (5%)
    all_gather x1, waiting for transfers between devices, local(): lax.all_gather(attn, 'tp', axis=1, tiled=True)  56.6 us
    all_to_all x1, waiting for transfers between devices, local(): lax.all_to_all(merged_accum.reshape(groups, per_group, TREE, local_cols),...  51.7 us
    ppermute x2, waiting for transfers between devices, swapped(): return lax.ppermute(value, axis, pairs)  31.8 us
    mul x3, local copies, waits for them, and re-layouts, combine_parts(): accum_first.reshape(split_shape) * factor_first[..., None]  15.5 us
    mul x3, local copies, waits for them, and re-layouts, combine_parts(): accum_second.reshape(split_shape) * factor_second[..., None]  15.4 us
    dot_general x6, matrix products, attend_part(): lax.dot_general(query_rows[:, :, lower:upper], key_rows[:, :, lower:upper...  14.7 us
    dot_general x6, matrix products, attend_part(): lax.dot_general(raw_weights.astype(jnp.bfloat16), value_rows[:, :, lower:...  12.4 us
    all_to_all x1, starting transfers between devices, local(): lax.all_to_all(outbound, 'rep', split_axis=0, concat_axis=0, tiled=True)  10.7 us
  transfers between devices with their start and end apart: 7, of which 4 were waited for; matrix products, arithmetic and copies ran while one was open for 20% of the time, Pallas kernels for 0%

commit v1 on v0

--- a/solution.py
+++ b/solution.py
@@ -1,3 +1,4 @@
+import functools
 import math
 import jax
 import jax.numpy as jnp
@@ -8,6 +9,16 @@
 TREE = 48
 PCAP = 152
 NEG_FILL = -1e30
+
+
+def attach_task_by_axis(in_array, across):
+    out_arr = jnp.concatenate(
+        lax.all_to_all(jnp.stack([in_array] * lax.axis_size(across), axis=0), across, 0, 0), axis=1
+    )
+    return out_arr
+
+
+show_the_flows = functools.partial(attach_task_by_axis, across="tp")
 
 
 def swapped(value, axis, apart):
@@ -139,11 +150,7 @@
     final_max, final_total, final_accum = combine_parts(remote_part, tree_part, HD)
     attn = final_accum.reshape(req_here, TREE, heads_here, HD) / final_total[..., None]
     attn = attn.reshape(req_here * TREE, local_cols).astype(jnp.bfloat16)
-    summed = jnp.dot(
-        lax.all_gather(attn, "tp", axis=1, tiled=True),
-        out_weight,
-        preferred_element_type=jnp.float32,
-    )
+    summed = jnp.dot(show_the_flows(attn), out_weight, preferred_element_type=jnp.float32)
     projected = summed.astype(jnp.bfloat16).reshape(req_here, TREE, out_weight.shape[1])
     accepted_cache = jnp.take_along_axis(tree_cache, accepted_path[:, None, :, None], axis=2)
     return (projected, accepted_cache)

time: 321 us -> 387 us (1.21)
  waiting for transfers between devices: 141 us -> 197 us
  starting transfers between devices: 42.5 us -> 57.7 us
  between operations: 15.8 us -> 2.45 us
  local copies, waits for them, and re-layouts: 63.3 us -> 73.7 us
    all_to_all x0 -> x1, waiting for transfers between devices: none -> 111 us  [attach_task_by_axis(): lax.all_to_all(jnp.stack([in_array] * lax.axis_size(across), axis=0), acr...]
    all_gather x1 -> x0, waiting for transfers between devices: 56.6 us -> none  [local(): lax.all_gather(attn, 'tp', axis=1, tiled=True)]
    all_to_all x0 -> x1, starting transfers between devices: none -> 15.4 us  [attach_task_by_axis(): lax.all_to_all(jnp.stack([in_array] * lax.axis_size(across), axis=0), acr...]
    reshape x0 -> x1, local copies, waits for them, and re-layouts: none -> 7.8 us  [attach_task_by_axis(): jnp.concatenate(lax.all_to_all(jnp.stack([in_array] * lax.axis_size(acros...]
  transfers between devices with their start and end apart: 7 -> 7, of which waited for: 4 -> 4; matrix products, arithmetic and copies ran while one was open for 20% -> 16% of each run, Pallas kernels for 0% -> 0%
where the time goes in v1:
time: 387 us; the launch traced here: 385 us
  waiting for transfers between devices  197 us (51%)
  local copies, waits for them, and re-layouts  73.7 us (19%)
  starting transfers between devices  57.7 us (15%)
  matrix products  32.5 us (8%)
  other arithmetic  22 us (6%)
    all_to_all x1, waiting for transfers between devices, attach_task_by_axis(): lax.all_to_all(jnp.stack([in_array] * lax.axis_size(across), axis=0), acr...  111 us
    all_to_all x1, waiting for transfers between devices, local(): lax.all_to_all(merged_accum.reshape(groups, per_group, TREE, local_cols),...  53 us
    ppermute x2, waiting for transfers between devices, swapped(): return lax.ppermute(value, axis, pairs)  31.8 us
    mul x3, local copies, waits for them, and re-layouts, combine_parts(): accum_first.reshape(split_shape) * factor_first[..., None]  15.5 us
    all_to_all x1, starting transfers between devices, attach_task_by_axis(): lax.all_to_all(jnp.stack([in_array] * lax.axis_size(across), axis=0), acr...  15.4 us
    mul x3, local copies, waits for them, and re-layouts, combine_parts(): accum_second.reshape(split_shape) * factor_second[..., None]  15.4 us
    dot_general x6, matrix products, attend_part(): lax.dot_general(query_rows[:, :, lower:upper], key_rows[:, :, lower:upper...  13.6 us
    dot_general x6, matrix products, attend_part(): lax.dot_general(raw_weights.astype(jnp.bfloat16), value_rows[:, :, lower:...  12.4 us
  transfers between devices with their start and end apart: 7, of which 4 were waited for; matrix products, arithmetic and copies ran while one was open for 16% of the time, Pallas kernels for 0%

profile of v1, /device:TPU:1, one launch (start us, length us, event | category | flops | bytes accessed | tf_op | source)
XLA Modules:
  0.0 385.0 jit_solution(6946388776180838661)
XLA Ops:
  0.6 1.0 convert_reduce_fusion
  1.6 1.1 compare_and_fusion.1
  2.8 1.7 convolution_convert_fusion
  4.5 2.0 copy.135
  6.5 10.7 %all-to-all-start = ((bf16[32,2,48,256]{3,2,1,0:T(8,128)(2,1)}), bf16[32,2,48,256]{3,2,1,0:T(8,128)(2,1)}, u32[]{:S(2)}, u32[]{:S(2)}) async-start(bf16[32,2,48,256]{3,2,1,0:T(8,128)(2,1)} %bitcast.165), calls=%async_computation | async-start | bytes 3145728 | tf_op jit(solution)/shard_map/all_to_all | solution.py:110
  17.3 3.1 collective-permute-start.1
  21.0 2.2 collective-permute-start
  23.9 31.8 %collective-permute-done = bf16[152]{0:T(256)(128)(2,1)S(1)} collective-permute-done((bf16[152]{0:T(256)(128)(2,1)S(1)}, bf16[152]{0:T(256)(128)(2,1)S(1)}, u32[]{:S(2)}, u32[]{:S(2)}) %collective-permute-start) | collective-permute-done | bytes 336 | tf_op jit(solution)/shard_map/ppermute | solution.py:27
  55.7 3.1 fusion.59
  58.8 3.1 fusion.60
  61.9 3.1 fusion.57
  65.0 3.0 fusion.58
  68.2 3.8 fusion.9
  72.0 2.5 copy.103
  74.4 1.6 copy.102
  76.0 3.3 fusion.38
  79.3 1.7 fusion.39
  81.2 3.7 fusion.5
  84.9 2.5 copy.100
  87.4 1.5 copy.99
  90.3 9.2 %all-to-all-start.2 = ((f32[32,1,192]{2,1,0:T(1,128)}), f32[32,1,192]{2,1,0:T(1,128)S(1)}, u32[]{:S(2)}, u32[]{:S(2)}) async-start(f32[32,1,192]{2,1,0:T(1,128)} %reshape.521), calls=%async_computation.2 | async-start | bytes 65536 | tf_op jit(solution)/shard_map/all_to_all | solution.py:121
  99.5 3.3 fusion.40
  102.9 1.7 fusion.41
  104.6 1.7 copy.101
  106.2 8.1 %mul.109 = f32[3072,2,128]{2,1,0:T(2,128)} broadcast(f32[3072,2]{1,0:T(8,128)} %copy.101), dimensions={0,1} | broadcast | bytes 3170304 | tf_op jit(solution)/shard_map/mul | solution.py:74
  114.4 5.5 %mul.110 = f32[32,2,48,256]{3,2,1,0:T(8,128)} reshape(f32[3072,2,128]{2,1,0:T(2,128)} %mul.109) | data formatting | bytes 6291456 | tf_op jit(solution)/shard_map/mul | solution.py:74
  119.9 1.7 copy.104
  121.6 8.1 %mul.112 = f32[3072,2,128]{2,1,0:T(2,128)} broadcast(f32[3072,2]{1,0:T(8,128)} %copy.104), dimensions={0,1} | broadcast | bytes 3170304 | tf_op jit(solution)/shard_map/mul | solution.py:75
  129.7 5.5 %mul.113 = f32[32,2,48,256]{3,2,1,0:T(8,128)} reshape(f32[3072,2,128]{2,1,0:T(2,128)} %mul.112) | data formatting | bytes 6291456 | tf_op jit(solution)/shard_map/mul | solution.py:75
  136.0 9.1 %all-to-all-start.3 = ((f32[32,1,192]{2,1,0:T(1,128)}), f32[32,1,192]{2,1,0:T(1,128)S(1)}, u32[]{:S(2)}, u32[]{:S(2)}) async-start(f32[32,1,192]{2,1,0:T(1,128)} %reshape.523), calls=%async_computation.3 | async-start | bytes 65536 | tf_op jit(solution)/shard_map/all_to_all | solution.py:128
  145.1 7.4 %fusion.4 = f32[32,2,48,256]{3,2,1,0:T(8,128)} fusion(f32[32,2,48,256]{3,2,1,0:T(8,128)} %mul.110, f32[32,2,48,128]{3,2,1,0:T(8,128)} %fusion.40, f32[32,2,48,128]{3,2,1,0:T(8,128)} %fusion.41, f32[32,2,48,256]{3,2,1,0:T(8,128)} %mul.113, f32[32,2,48,128]{3,2,1,0:T(8,128)} %fusion.38, f32[32,2,48,128]{3,2,1,0:T(8,128)} %fusion.39), kind=kLoop, calls=%fused_computation.13 | loop fusion | flops 3932160 | bytes 15728640 | tf_op jit(solution)/shard_map/add | solution.py:74
  152.5 1.4 all-to-all-done.3
  154.5 8.0 %all-to-all-start.1 = ((f32[32,2,48,256]{3,2,1,0:T(8,128)}), f32[32,2,48,256]{3,2,1,0:T(8,128)}, u32[]{:S(2)}, u32[]{:S(2)}) async-start(f32[32,2,48,256]{3,2,1,0:T(8,128)} %fusion.4), calls=%async_computation.1 | async-start | bytes 6291456 | tf_op jit(solution)/shard_map/all_to_all | solution.py:135
  162.8 1.1 fusion.55
  168.1 1.2 fusion.22
  169.3 1.2 fusion.24
  172.0 1.5 reduce.16
  178.3 0.9 copy.117
  180.1 53.0 %all-to-all-done.1 = f32[32,2,48,256]{3,2,1,0:T(8,128)} async-done(((f32[32,2,48,256]{3,2,1,0:T(8,128)}), f32[32,2,48,256]{3,2,1,0:T(8,128)}, u32[]{:S(2)}, u32[]{:S(2)}) %all-to-all-start.1) | async-done | bytes 3145760 | tf_op jit(solution)/shard_map/all_to_all | solution.py:135
  233.1 3.4 gather_fusion
  236.5 1.8 mul.117
  238.3 1.7 mul.120
  241.2 2.6 stack.109
  243.8 15.4 %all-to-all-start.4 = ((bf16[16,624,256]{2,1,0:T(8,128)(2,1)}), bf16[16,624,256]{2,1,0:T(8,128)(2,1)}, u32[]{:S(2)}, u32[]{:S(2)}) async-start(bf16[16,624,256]{2,1,0:T(8,128)(2,1)} %stack.109), calls=%async_computation.4 | async-start | bytes 10223616 | tf_op jit(solution)/shard_map/all_to_all | solution.py:16
  259.4 1.6 gather_fusion.1
  261.9 110.5 %all-to-all-done.4 = bf16[16,624,256]{2,1,0:T(8,128)(2,1)} async-done(((bf16[16,624,256]{2,1,0:T(8,128)(2,1)}), bf16[16,624,256]{2,1,0:T(8,128)(2,1)}, u32[]{:S(2)}, u32[]{:S(2)}) %all-to-all-start.4) | async-done | bytes 5111840 | tf_op jit(solution)/shard_map/all_to_all | solution.py:16
  372.4 7.8 %copy.125 = bf16[624,16,256]{0,2,1:T(8,128)(2,1)} copy(bf16[624,16,256]{2,0,1:T(8,128)(2,1)} %bitcast.46) | data formatting | bytes 10223616 | tf_op jit(solution)/shard_map/reshape | solution.py:15
  380.3 4.8 %convolution_convert_fusion.1 = bf16[624,256]{1,0:T(8,128)(2,1)} fusion(bf16[624,4096]{0,1:T(8,128)(2,1)} %bitcast.164, bf16[4096,256]{1,0:T(8,128)(2,1)S(1)} %copy-done), kind=kOutput, calls=%fused_computation.28 | convolution fusion | flops 1308782592 | bytes 7528448 | tf_op jit(solution)/shard_map/dot_general | solution.py:153
  (97 shorter events, 16.9 us)
Async XLA Ops:
  0.6 379.6 %copy-start = (bf16[4096,256]{1,0:T(8,128)(2,1)S(1)}, bf16[4096,256]{1,0:T(8,128)(2,1)}, u32[]{:S(2)}) copy-start(bf16[4096,256]{1,0:T(8,128)(2,1)} %param.21) | copy-start | bytes 6291460
  6.5 10.8 %copy-start.15 = (bf16[1,2,152,256]{3,2,1,0:T(8,128)(2,1)S(1)}, bf16[1,2,152,256]{3,2,1,0:T(8,128)(2,1)}, u32[]{:S(2)}) copy-start(bf16[1,2,152,256]{3,2,1,0:T(8,128)(2,1)} %param.19) | copy-start | bytes 466948
  6.5 17.4 %copy-start.10 = (bf16[1,2,152,256]{3,2,1,0:T(8,128)(2,1)S(1)}, bf16[1,2,152,256]{3,2,1,0:T(8,128)(2,1)}, u32[]{:S(2)}) copy-start(bf16[1,2,152,256]{3,2,1,0:T(8,128)(2,1)} %param.17) | copy-start | bytes 466948
  6.5 49.2 %all-to-all-start = ((bf16[32,2,48,256]{3,2,1,0:T(8,128)(2,1)}), bf16[32,2,48,256]{3,2,1,0:T(8,128)(2,1)}, u32[]{:S(2)}, u32[]{:S(2)}) async-start(bf16[32,2,48,256]{3,2,1,0:T(8,128)(2,1)} %bitcast.165), calls=%async_computation | async-start | bytes 3145728 | tf_op jit(solution)/shard_map/all_to_all | solution.py:110
  17.3 38.4 %collective-permute-start.1 = (bf16[1,2,152,256]{3,2,1,0:T(8,128)(2,1)S(1)}, bf16[1,2,152,256]{3,2,1,0:T(8,128)(2,1)S(1)}, u32[]{:S(2)}, u32[]{:S(2)}) collective-permute-start(bf16[1,2,152,256]{3,2,1,0:T(8,128)(2,1)S(1)} %copy-done.15), channel_id=1, source_target_pairs={{0,16},{16,0},{32,48},{48,32},{64,80},{80,64},{96,112},{112,96},{1... | collective-permute-start | bytes 466952 | tf_op jit(solution)/shard_map/ppermute | solution.py:27
  21.0 34.7 %collective-permute-start = (bf16[152]{0:T(256)(128)(2,1)S(1)}, bf16[152]{0:T(256)(128)(2,1)S(1)}, u32[]{:S(2)}, u32[]{:S(2)}) collective-permute-start(bf16[152]{0:T(256)(128)(2,1)S(1)} %compare_convert_fusion), channel_id=1, source_target_pairs={{0,16},{16,0},{32,48},{48,32},{64,80},{80,64},{96,112},{112,96},{1... | collective-permute-start | bytes 920 | tf_op jit(solution)/shard_map/ppermute | solution.py:27
  76.0 3.3 copy-start.2
  90.3 45.7 %all-to-all-start.2 = ((f32[32,1,192]{2,1,0:T(1,128)}), f32[32,1,192]{2,1,0:T(1,128)S(1)}, u32[]{:S(2)}, u32[]{:S(2)}) async-start(f32[32,1,192]{2,1,0:T(1,128)} %reshape.521), calls=%async_computation.2 | async-start | bytes 65536 | tf_op jit(solution)/shard_map/all_to_all | solution.py:121
  99.5 3.4 copy-start.1
  136.0 17.8 %all-to-all-start.3 = ((f32[32,1,192]{2,1,0:T(1,128)}), f32[32,1,192]{2,1,0:T(1,128)S(1)}, u32[]{:S(2)}, u32[]{:S(2)}) async-start(f32[32,1,192]{2,1,0:T(1,128)} %reshape.523), calls=%async_computation.3 | async-start | bytes 65536 | tf_op jit(solution)/shard_map/all_to_all | solution.py:128
  152.5 10.0 %copy-start.9 = (s32[13,48,48]{2,1,0:T(8,128)S(1)}, s32[13,48,48]{2,1,0:T(8,128)}, u32[]{:S(2)}) copy-start(s32[13,48,48]{2,1,0:T(8,128)} %param.14) | copy-start | bytes 359428
  152.5 10.2 %copy-start.3 = (bf16[13,2,48,256]{3,2,1,0:T(8,128)(2,1)S(1)}, bf16[13,2,48,256]{3,2,1,0:T(8,128)(2,1)}, u32[]{:S(2)}) copy-start(bf16[13,2,48,256]{3,2,1,0:T(8,128)(2,1)} %param.13) | copy-start | bytes 1916932
  153.9 0.6 copy-start.11
  154.5 78.6 %all-to-all-start.1 = ((f32[32,2,48,256]{3,2,1,0:T(8,128)}), f32[32,2,48,256]{3,2,1,0:T(8,128)}, u32[]{:S(2)}, u32[]{:S(2)}) async-start(f32[32,2,48,256]{3,2,1,0:T(8,128)} %fusion.4), calls=%async_computation.1 | async-start | bytes 6291456 | tf_op jit(solution)/shard_map/all_to_all | solution.py:135
  162.6 1.3 copy-start.8
  162.7 3.4 copy-start.14
  163.9 0.7 copy-start.5
  164.2 0.7 copy-start.6
  233.1 7.9 %copy-start.13 = (pred[624]{0:T(1024)(128)(4,1)S(1)}, pred[624]{0:T(1024)(128)(4,1)}, u32[]{:S(2)}) copy-start(pred[624]{0:T(1024)(128)(4,1)} %broadcast_in_dim.103) | copy-start | bytes 1876
  236.5 3.6 copy-start.7
  236.5 4.4 %copy-start.4 = (f32[13,48,256]{2,1,0:T(8,128)S(1)}, f32[13,48,256]{2,1,0:T(8,128)}, u32[]{:S(2)}) copy-start(f32[13,48,256]{2,1,0:T(8,128)} %gather_fusion) | copy-start | bytes 1916932
  243.8 15.4 %copy-start.12 = (s32[13,8]{0,1:T(8,128)S(1)}, s32[13,8]{0,1:T(8,128)}, u32[]{:S(2)}) copy-start(s32[13,8]{0,1:T(8,128)} %param.16) | copy-start | bytes 1252
  243.8 128.6 %all-to-all-start.4 = ((bf16[16,624,256]{2,1,0:T(8,128)(2,1)}), bf16[16,624,256]{2,1,0:T(8,128)(2,1)}, u32[]{:S(2)}, u32[]{:S(2)}) async-start(bf16[16,624,256]{2,1,0:T(8,128)(2,1)} %stack.109), calls=%async_computation.4 | async-start | bytes 10223616 | tf_op jit(solution)/shard_map/all_to_all | solution.py:16
